TPU v7x, 512 devices: a whole 4x4x16 slice. The times are simulated.
512 devices in a mesh: row: 64 (over z_lo, y, x), col: 8 (over z_hi, core).
Axes of the slice: x: 4, y: 4, z: 16 (z_hi: 4, z_lo: 4; z = z_hi * 4 + z_lo), core: 2. Of those that a mesh axis runs over, the one named last changes fastest.
Arguments:
- front: float32 [65536, 1024], P('row', 'col'), may hold values from -6 to 6
- contrib: bfloat16 [524288, 1024], P('row', 'col'), may hold values from -6 to 6
- target: int32 [2048], replicated, may hold values from 0 to 255, as said below
- mask: int32 [256, 8], P('row', 'col'), may hold values 0 or 1
- panel: float32 [65536, 256], P(('row', 'col')), as said below
- pivots: int32 [256], replicated, may hold values from 0 to 65535, as said below
Outputs:
- lower: float32 [65536, 256], P(('row', 'col'))
- schur: float32 [65536, 1024], P('row', 'col')
Inputs may be any that keep to these rules, and one draw needn't show every extreme that they name: Front block row t lies on index t // 4 of row. Within each aligned block of 32 entries (one device's contribution blocks) the values target // 4 are distinct, and index 0 of row receives a block from every aligned block. `pivots`: distinct rows; each aligned group of 1024 rows holds exactly 4 of them. The 256 x 256 matrix formed by the panel's rows named in pivots is invertible.
All inputs are finite; a program needn't handle non-finite values. No bound on the sum of `mask` on one device may be relied on, other than what follows from the above.
Results may differ from a plain program's by a relative error of at most 0.0003.
Values may be sent and summed in bfloat16 or wider, within the bound.
No kernel may reach another device: no remote copies, remote signals or barrier semaphores. Data moves between devices by JAX's collectives and lax.ppermute only.
A program may use at most 64 MiB of HBM per device.

v0:
```python
import jax
import jax.numpy as jnp
from jax import lax
from jax.sharding import PartitionSpec as P

BLK = 256


def exact_dot(left, right):
    return jnp.dot(left, right, precision=lax.Precision.HIGHEST, preferred_element_type=jnp.float32)


def body(front, contrib, target, mask, panel, pivots):
    row_count = lax.axis_size("row")
    col_count = lax.axis_size("col")
    row_index = lax.axis_index("row")
    col_index = lax.axis_index("col")
    tile_rows, tile_cols = front.shape
    blocks_own = tile_rows // BLK
    sent_count = contrib.shape[0] // BLK
    targets = target.reshape(row_count, sent_count)
    own_targets = lax.dynamic_slice_in_dim(targets, row_index, 1, 0)[0]
    device_ids = jnp.arange(row_count, dtype=jnp.int32)
    chooser = (own_targets[None, :] // blocks_own == device_ids[:, None]).astype(jnp.bfloat16)
    pieces = contrib.reshape(sent_count, BLK, tile_cols)
    outgoing = jnp.einsum(
        "db,bxc->dxc", chooser, pieces, preferred_element_type=jnp.float32
    ).astype(jnp.bfloat16)
    arrived = lax.all_to_all(outgoing, "row", split_axis=0, concat_axis=0, tiled=True)
    source_targets = jnp.take(targets, device_ids, axis=0)
    block_ids = jnp.arange(blocks_own, dtype=jnp.int32)
    own_blocks = row_index * blocks_own + block_ids
    placing = jnp.sum(
        (source_targets[:, :, None] == own_blocks[None, None, :]).astype(jnp.float32), axis=1
    ).astype(jnp.bfloat16)
    added = jnp.einsum("sk,sxc->kxc", placing, arrived, preferred_element_type=jnp.float32).reshape(
        tile_rows, tile_cols
    )
    assembled = front + added
    panel_rows = panel.shape[0]
    panel_start = (row_index * col_count + col_index) * panel_rows
    select_rows = (
        pivots[:, None] - panel_start == jnp.arange(panel_rows, dtype=jnp.int32)[None, :]
    ).astype(jnp.float32)
    pivot_block = lax.psum(exact_dot(select_rows, panel), ("row", "col"))
    gram = exact_dot(pivot_block, pivot_block.T)
    factor_low = jnp.linalg.cholesky(gram)
    inverse = jax.scipy.linalg.cho_solve((factor_low, True), pivot_block).T
    local_start = row_index * tile_rows
    picker = (
        pivots[:, None] - local_start == jnp.arange(tile_rows, dtype=jnp.int32)[None, :]
    ).astype(jnp.float32)
    upper = lax.psum(exact_dot(picker, assembled), "row")
    lower_own = exact_dot(panel, inverse)
    update = exact_dot(lax.all_gather(lower_own, "col", axis=0, tiled=True), upper)
    row_mask = jnp.repeat(mask[:, 0].astype(jnp.float32), BLK)
    schur = assembled - row_mask[:, None] * update
    return (lower_own, schur)


def solution(mesh):
    placed = (P("row", "col"), P("row", "col"), P(), P("row", "col"), P(("row", "col"), None), P())
    return jax.shard_map(
        body,
        mesh=mesh,
        in_specs=placed,
        out_specs=(P(("row", "col"), None), P("row", "col")),
        check_vma=False,
    )
```

profile of v0, /device:TPU:2, one launch (start us, length us, event | category | flops | bytes accessed | tf_op | source)
XLA Modules:
  0.0 1228.4 jit_solution(2532103232973570547)
XLA Ops:
  8.0 0.9 reshape.68
  8.9 0.7 copy-done
  9.6 1.8 convolution_convert_fusion
  11.4 4.7 copy.22
  16.1 12.4 %all-to-all-start = ((bf16[64,256,128]{2,1,0:T(8,128)(2,1)}), bf16[64,256,128]{2,1,0:T(8,128)(2,1)}, u32[]{:S(2)}, u32[]{:S(2)}) async-start(bf16[64,256,128]{2,1,0:T(8,128)(2,1)} %copy.22), calls=%async_computation | async-start | bytes 8388608 | tf_op jit(solution)/shard_map/all_to_all | solution.py:29
  28.5 0.0 all-reduce.4.cloned.1.call-start
  28.6 1.0 fusion.12
  29.6 0.0 all-reduce.4.cloned.1.call-update
  29.7 0.2 all-gather.2.cloned.1.call-start
  29.9 474.1 %all-reduce.4.cloned.1.call-done = f32[256,256]{1,0:T(8,128)} async-done(((f32[256,256]{1,0:T(8,128)}), f32[256,256]{1,0:T(8,128)}) %all-reduce.4.cloned.1.call-update) | async-done | bytes 262160 | tf_op jit(solution)/shard_map/psum | solution.py:45
  504.0 1.5 fusion.30
  505.5 0.1 copy.19
  505.7 11.7 cholesky.50
  517.5 9.8 custom-call.18
  527.3 0.2 constant_dynamic-update-slice_fusion
  527.5 0.3 convolution_subtract_fusion.2
  527.7 11.7 cholesky.105
  539.5 0.7 compare_reduce_fusion
  541.6 0.1 triangular_solve.66
  541.6 4.2 while.1
  541.8 0.6 fusion.46
  542.4 1.4 bitcast_dynamic-update-slice_fusion.2
  543.9 0.6 fusion.46
  544.5 1.4 bitcast_dynamic-update-slice_fusion.2
  545.9 0.6 copy-done.6
  546.5 20.5 %custom-call.19 = f32[2,128,128]{1,2,0:T(8,128)S(1)} custom-call(f32[2,128,128]{2,1,0:T(8,128)} %copy-done.6), custom_call_target="InvertDiagBlocksLowerTriangular" | custom-call | tf_op jit(solution)/shard_map/jit(_cho_solve)/triangular_solve | solution.py:48
  567.0 0.3 fusion.10
  567.4 0.3 convolution_subtract_fusion.1
  567.6 0.3 fusion.19
  568.0 0.3 fusion.18
  568.2 0.3 convolution_subtract_fusion
  568.5 0.3 fusion.17
  568.8 1.0 convolution_bitcast_fusion
  569.8 0.0 all-gather.2.cloned.1.call-update
  569.9 0.0 all-reduce.6.cloned.1.call-start
  569.9 0.6 gather_fusion
  570.6 0.1 broadcast_select_fusion
  570.6 0.1 copy.20
  570.7 0.1 convert_reduce_fusion
  570.8 4.5 fusion
  575.4 0.1 bitcast_add_fusion
  575.5 1.3 fusion.4
  576.8 0.0 all-reduce.6.cloned.1.call-update
  576.9 0.1 broadcast_bitcast_fusion
  576.9 0.8 copy.25
  577.7 41.3 %all-gather.2.cloned.1.call-done = f32[1024,256]{0,1:T(8,128)} async-done(((f32[128,256]{0,1:T(8,128)}), f32[1024,256]{0,1:T(8,128)}) %all-gather.2.cloned.1.call-update) | async-done | bytes 1048592 | tf_op jit(solution)/shard_map/all_gather | solution.py:55
  619.0 598.1 %all-reduce.6.cloned.1.call-done = f32[256,128]{1,0:T(8,128)} async-done(((f32[256,128]{1,0:T(8,128)}), f32[256,128]{1,0:T(8,128)}) %all-reduce.6.cloned.1.call-update) | async-done | bytes 131088 | tf_op jit(solution)/shard_map/psum | solution.py:53
  1217.1 3.9 fusion.3
  (34 shorter events, 0.3 us)
Async XLA Ops:
  8.0 1.6 copy-start
  16.1 12.5 %copy-start.5 = (s32[256]{0:T(256)S(1)}, s32[256]{0:T(256)}, u32[]{:S(2)}) copy-start(s32[256]{0:T(256)} %param.11) | copy-start | bytes 3076
  16.1 12.5 %copy-start.4 = (f32[128,256]{1,0:T(8,128)S(1)}, f32[128,256]{1,0:T(8,128)}, u32[]{:S(2)}) copy-start(f32[128,256]{1,0:T(8,128)} %param.10) | copy-start | bytes 393220
  16.1 554.7 %all-to-all-start = ((bf16[64,256,128]{2,1,0:T(8,128)(2,1)}), bf16[64,256,128]{2,1,0:T(8,128)(2,1)}, u32[]{:S(2)}, u32[]{:S(2)}) async-start(bf16[64,256,128]{2,1,0:T(8,128)(2,1)} %copy.22), calls=%async_computation | async-start | bytes 8388608 | tf_op jit(solution)/shard_map/all_to_all | solution.py:29
  28.5 475.4 %all-reduce.4.cloned.1.call-start = ((), (), s32[]{:S(2)}) async-start(), calls=%async_computation.1 | async-start | bytes 524288 | tf_op jit(solution)/shard_map/psum | solution.py:45
  29.6 541.2 %copy-start.7 = (s32[4,1]{0,1:T(1,128)S(1)}, s32[4,1]{0,1:T(1,128)}, u32[]{:S(2)}) copy-start(s32[4,1]{0,1:T(1,128)} %param.9) | copy-start | bytes 52
  29.7 589.3 %all-gather.2.cloned.1.call-start = ((), (), s32[]{:S(2)}) async-start(), calls=%async_computation.2 | async-start | bytes 1179648 | tf_op jit(solution)/shard_map/all_gather | solution.py:55
  504.0 63.1 %copy-start.1 = (f32[256,256]{1,0:T(8,128)S(1)}, f32[256,256]{1,0:T(8,128)}, u32[]{:S(2)}) copy-start(f32[256,256]{1,0:T(8,128)} %all-reduce.4.cloned.1.call-done) | copy-start | bytes 786436
  545.9 0.7 copy-start.6
  567.6 7.8 copy-start.3
  569.9 647.2 %all-reduce.6.cloned.1.call-start = ((), (), s32[]{:S(2)}) async-start(), calls=%async_computation.3 | async-start | bytes 262144 | tf_op jit(solution)/shard_map/psum | solution.py:53
  570.5 6.4 copy-start.2
Sparse Core Ops, SparseCore 0:
  35.4 468.5 all-reduce.3
  570.0 48.9 all-gather.1
Sparse Core Ops, SparseCore 1:
  576.9 640.1 all-reduce.5
where the time goes:
time: 1230 us
  waiting for transfers between devices  1110 us (90%)
  other arithmetic  54.8 us (4%)
  matrix products  17.3 us (1%)
  between operations  17.1 us (1%)
  local copies, waits for them, and re-layouts  12.7 us (1%)
  starting transfers between devices  12.7 us (1%)
    psum x1, waiting for transfers between devices, body(): upper = lax.psum(exact_dot(picker, assembled), 'row')  598 us
    psum x1, waiting for transfers between devices, body(): pivot_block = lax.psum(exact_dot(select_rows, panel), ('row', 'col'))  474 us
    all_gather x1, waiting for transfers between devices, body(): lax.all_gather(lower_own, 'col', axis=0, tiled=True)  41.3 us
    another operation x6, other arithmetic, body(): factor_low = jnp.linalg.cholesky(gram)  34 us
  transfers between devices with their start and end apart: 4, of which 3 were waited for; matrix products, arithmetic and copies ran while one was open for 6% of the time, Pallas kernels for 0%

commit v1 on v0

--- a/solution.py
+++ b/solution.py
@@ -42,7 +42,7 @@
     select_rows = (
         pivots[:, None] - panel_start == jnp.arange(panel_rows, dtype=jnp.int32)[None, :]
     ).astype(jnp.float32)
-    pivot_block = lax.psum(exact_dot(select_rows, panel), ("row", "col"))
+    pivot_block = lax.psum(lax.psum(exact_dot(select_rows, panel), "row"), "col")
     gram = exact_dot(pivot_block, pivot_block.T)
     factor_low = jnp.linalg.cholesky(gram)
     inverse = jax.scipy.linalg.cho_solve((factor_low, True), pivot_block).T

time: 1230 us -> 1050 us (0.85)
  the two profiles are of different devices: /device:TPU:2 before, /device:TPU:97 now
where the time goes in v1:
time: 1050 us
  waiting for transfers between devices  934 us (89%)
  other arithmetic  54.8 us (5%)
  matrix products  19 us (2%)
  between operations  15.3 us (1%)
  local copies, waits for them, and re-layouts  14.8 us (1%)
  starting transfers between devices  11 us (1%)
    psum x1, waiting for transfers between devices, body(): lax.psum(exact_dot(select_rows, panel), 'row')  634 us
    psum x1, waiting for transfers between devices, body(): lax.psum(lax.psum(exact_dot(select_rows, panel), 'row'), 'col')  159 us
    all_to_all x1, waiting for transfers between devices, body(): lax.all_to_all(outgoing, 'row', split_axis=0, concat_axis=0, tiled=True)  89.6 us
    all_gather x1, waiting for transfers between devices, body(): lax.all_gather(lower_own, 'col', axis=0, tiled=True)  52.1 us
    another operation x6, other arithmetic, body(): factor_low = jnp.linalg.cholesky(gram)  34 us
  transfers between devices with their start and end apart: 4, of which 4 were waited for; matrix products, arithmetic and copies ran while one was open for 0% of the time, Pallas kernels for 0%

profile of v1, /device:TPU:97, one launch (start us, length us, event | category | flops | bytes accessed | tf_op | source)
XLA Modules:
  0.0 1049.5 jit_solution(17896690102860368113)
XLA Ops:
  7.2 0.9 reshape.68
  8.1 0.7 copy-done
  8.8 1.8 convolution_convert_fusion
  10.6 4.7 copy.22
  15.3 10.7 %all-to-all-start = ((bf16[64,256,128]{2,1,0:T(8,128)(2,1)}), bf16[64,256,128]{2,1,0:T(8,128)(2,1)}, u32[]{:S(2)}, u32[]{:S(2)}) async-start(bf16[64,256,128]{2,1,0:T(8,128)(2,1)} %copy.22), calls=%async_computation | async-start | bytes 8388608 | tf_op jit(solution)/shard_map/all_to_all | solution.py:29
  26.0 0.0 all-reduce.7.cloned.1.call-start
  26.1 0.6 gather_fusion
  26.7 0.1 broadcast_select_fusion
  26.8 0.1 copy.20
  26.8 0.1 convert_reduce_fusion
  27.0 1.0 fusion.12
  28.0 89.6 %all-to-all-done = bf16[64,256,128]{2,1,0:T(8,128)(2,1)} async-done(((bf16[64,256,128]{2,1,0:T(8,128)(2,1)}), bf16[64,256,128]{2,1,0:T(8,128)(2,1)}, u32[]{:S(2)}, u32[]{:S(2)}) %all-to-all-start) | async-done | bytes 4194336 | tf_op jit(solution)/shard_map/all_to_all | solution.py:29
  117.6 4.5 fusion
  122.1 0.1 bitcast_add_fusion
  122.2 1.3 fusion.4
  123.5 0.0 all-reduce.7.cloned.1.call-update
  123.6 0.0 all-reduce.5.cloned.1.call-start
  123.6 633.5 %all-reduce.7.cloned.1.call-done = (f32[256,256]{1,0:T(8,128)}, f32[256,128]{1,0:T(8,128)}) async-done(((f32[256,256]{1,0:T(8,128)}, f32[256,128]{1,0:T(8,128)}), (f32[256,256]{1,0:T(8,128)}, f32[256,128]{1,0:T(8,128)})) %all-reduce.7.cloned.1.call-update) | async-done | bytes 393232 | tf_op jit(solution)/shard_map/psum | solution.py:45
  757.1 0.0 all-reduce.5.cloned.1.call-update
  757.1 0.2 all-gather.2.cloned.1.call-start
  757.4 159.2 %all-reduce.5.cloned.1.call-done = f32[256,256]{1,0:T(8,128)} async-done(((f32[256,256]{1,0:T(8,128)}), f32[256,256]{1,0:T(8,128)}) %all-reduce.5.cloned.1.call-update) | async-done | bytes 262160 | tf_op jit(solution)/shard_map/psum | solution.py:45
  916.6 1.5 fusion.30
  918.1 0.1 copy.19
  918.3 0.7 copy-done.2
  919.0 11.7 %cholesky.50 = f32[128,128]{1,0:T(8,128)S(1)} custom-call(f32[128,128]{1,0:T(8,128)S(1)} %cholesky.118), custom_call_target="Cholesky" | custom-call | tf_op jit(solution)/shard_map/jit(cholesky)/cholesky | solution.py:47
  930.8 9.8 custom-call.18
  940.6 1.0 constant_dynamic-update-slice_fusion
  941.7 1.1 convolution_subtract_fusion.2
  942.8 11.7 %cholesky.105 = f32[128,128]{1,0:T(8,128)S(1)} custom-call(f32[128,128]{1,0:T(8,128)S(1)} %convolution_subtract_fusion.2), custom_call_target="Cholesky" | custom-call | tf_op jit(solution)/shard_map/jit(cholesky)/cholesky | solution.py:47
  954.5 0.7 compare_reduce_fusion
  956.5 0.1 triangular_solve.66
  956.6 5.4 while.1
  956.8 0.6 fusion.46
  957.4 2.0 bitcast_dynamic-update-slice_fusion.2
  959.4 0.6 fusion.46
  960.0 2.0 bitcast_dynamic-update-slice_fusion.2
  962.0 20.5 %custom-call.19 = f32[2,128,128]{1,2,0:T(8,128)S(1)} custom-call(f32[2,128,128]{2,1,0:T(8,128)} %get-tuple-element.9), custom_call_target="InvertDiagBlocksLowerTriangular" | custom-call | tf_op jit(solution)/shard_map/jit(_cho_solve)/triangular_solve | solution.py:48
  982.5 0.3 fusion.10
  982.8 0.3 convolution_subtract_fusion.1
  983.0 0.3 fusion.19
  983.4 0.3 fusion.18
  983.6 0.3 convolution_subtract_fusion
  984.0 0.3 fusion.17
  984.2 1.0 convolution_bitcast_fusion
  985.3 0.1 broadcast_bitcast_fusion
  985.4 1.7 copy.25
  987.0 52.1 %all-gather.2.cloned.1.call-done = f32[1024,256]{0,1:T(8,128)} async-done(((f32[128,256]{0,1:T(8,128)}), f32[1024,256]{0,1:T(8,128)}) %all-gather.2.cloned.1.call-update) | async-done | bytes 1048592 | tf_op jit(solution)/shard_map/all_gather | solution.py:55
  1039.2 3.9 fusion.3
  (32 shorter events, 0.3 us)
Async XLA Ops:
  7.2 1.6 copy-start
  15.3 11.7 %copy-start.5 = (s32[256]{0:T(256)S(1)}, s32[256]{0:T(256)}, u32[]{:S(2)}) copy-start(s32[256]{0:T(256)} %param.11) | copy-start | bytes 3076
  15.3 11.7 %copy-start.4 = (f32[128,256]{1,0:T(8,128)S(1)}, f32[128,256]{1,0:T(8,128)}, u32[]{:S(2)}) copy-start(f32[128,256]{1,0:T(8,128)} %param.10) | copy-start | bytes 393220
  15.3 102.3 %all-to-all-start = ((bf16[64,256,128]{2,1,0:T(8,128)(2,1)}), bf16[64,256,128]{2,1,0:T(8,128)(2,1)}, u32[]{:S(2)}, u32[]{:S(2)}) async-start(bf16[64,256,128]{2,1,0:T(8,128)(2,1)} %copy.22), calls=%async_computation | async-start | bytes 8388608 | tf_op jit(solution)/shard_map/all_to_all | solution.py:29
  26.0 96.1 %copy-start.3 = (f32[1024,128]{1,0:T(8,128)S(1)}, f32[1024,128]{1,0:T(8,128)}, u32[]{:S(2)}) copy-start(f32[1024,128]{1,0:T(8,128)} %param.6) | copy-start | bytes 1572868
  26.0 731.1 %all-reduce.7.cloned.1.call-start = ((), (), s32[]{:S(2)}) async-start(), calls=%async_computation.3 | async-start | bytes 786432 | tf_op jit(solution)/shard_map/psum | solution.py:45
  123.5 861.7 %copy-start.6 = (s32[4,1]{0,1:T(1,128)S(1)}, s32[4,1]{0,1:T(1,128)}, u32[]{:S(2)}) copy-start(s32[4,1]{0,1:T(1,128)} %param.9) | copy-start | bytes 52
  123.6 793.0 %all-reduce.5.cloned.1.call-start = ((), (), s32[]{:S(2)}) async-start(), calls=%async_computation.1 | async-start | bytes 524288 | tf_op jit(solution)/shard_map/psum | solution.py:45
  757.1 282.0 %all-gather.2.cloned.1.call-start = ((), (), s32[]{:S(2)}) async-start(), calls=%async_computation.2 | async-start | bytes 1179648 | tf_op jit(solution)/shard_map/all_gather | solution.py:55
  916.6 65.8 %copy-start.1 = (f32[256,256]{1,0:T(8,128)S(1)}, f32[256,256]{1,0:T(8,128)}, u32[]{:S(2)}) copy-start(f32[256,256]{1,0:T(8,128)} %all-reduce.5.cloned.1.call-done) | copy-start | bytes 786436
  918.3 0.7 copy-start.2
Sparse Core Ops, SparseCore 0:
  123.7 633.3 all-reduce.6
  760.3 156.2 all-reduce.4
  985.4 53.7 all-gather.1
